TPU v7x, 32 devices: a whole 2x2x4 slice. The times are simulated.
32 devices in a mesh: groups: 2 (over y), cell: 4 (over z), member: 4 (over x, core).
Axes of the slice: x: 2, y: 2, z: 4, core: 2. Of those that a mesh axis runs over, the one named last changes fastest.
Arguments:
- prior_sample_set: float32 [512, 3, 32, 512], P(('groups', 'member'), None, 'cell'), parts along dimension 0, may hold values from -6 to 6
- wind_table: float32 [8, 2], replicated, may hold values from -0.45 to 0.45
- regimes: int32 [16, 4], P('groups'), parts along dimension 0, may hold values from 0 to 7
- obs_index: int32 [8, 512], P(('groups', 'cell')), parts along dimension 0, may hold values from 0 to 4095
- obs_count: int32 [8], P(('groups', 'cell')), parts along dimension 0, may hold values from 1 to 512, as said below
- obs_value: float32 [8, 512], P(('groups', 'cell')), parts along dimension 0, may hold values from -6 to 6
- obs_var: float32 [8, 512], P(('groups', 'cell')), parts along dimension 0, may hold values from 0.25 to 4
Outputs:
- posterior_sample_set: float32 [512, 3, 32, 512], P(('groups', 'member'), None, 'cell'), parts along dimension 0
There are 2 independent parts, one for each index of `groups`. A program takes and returns all parts, laid end to end along the dimension named above; an argument that names none is the same for every part. Nothing has to cross between parts.
Inputs may be any that keep to these rules, and one draw needn't show every extreme that they name: `obs_count`: some tile has exactly 512 live slots.
All inputs are finite; a program needn't handle non-finite values.
Results may differ from a plain program's by a relative error of at most 0.019.
The roundings to bfloat16 on the way count: a program that leaves them out, or rounds other values in their place, can miss the bound.
Values may be sent and summed in bfloat16 or wider, within the bound.
A program may use at most 64 MiB of HBM per device.

v0:
```python
import jax
import jax.numpy as jnp
from jax import lax
from jax.sharding import PartitionSpec as P

SUBSTEPS = 4
BAND = 4
ROOT_STEPS = 24
diffusion = 0.02


def padded_2(cells, sides, width):
    for axis, dim in sides:
        count = lax.axis_size(axis)
        ends = count - 1
        head = lax.slice_in_dim(cells, 0, width, axis=dim)
        tail = lax.slice_in_dim(cells, cells.shape[dim] - width, cells.shape[dim], axis=dim)
        cells = jnp.concatenate(
            [
                lax.ppermute(tail, axis, [(i, (i + 1) % count) for i in range(ends)]),
                cells,
                lax.ppermute(head, axis, [((i + 1) % count, i) for i in range(ends)]),
            ],
            axis=dim,
        )
    return cells


def row_speeds(row_ids, regime_column, wind_table, row_total):
    band_ids = jnp.clip(row_ids, 0, row_total - 1) // BAND
    band_hits = (band_ids[:, None] == jnp.arange(regime_column.shape[0])[None, :]).astype(jnp.int32)
    regime_ids = jnp.sum(band_hits * regime_column[None, :], axis=1)
    regime_hits = (regime_ids[:, None] == jnp.arange(wind_table.shape[0])[None, :]).astype(
        jnp.float32
    )
    speed = jnp.dot(
        regime_hits, wind_table, precision=lax.Precision.HIGHEST, preferred_element_type=jnp.float32
    )
    return (speed[:, 0:1], speed[:, 1:2])


def stencil(padded, speed_x, speed_y):
    centre = padded[..., 1:-1, :]
    south = padded[..., :-2, :]
    north = padded[..., 2:, :]
    widths = [(0, 0)] * (centre.ndim - 1) + [(1, 1)]
    sides = jnp.pad(centre, widths)
    west = sides[..., :-2]
    east = sides[..., 2:]
    result = (
        centre
        - jnp.maximum(speed_x, 0.0) * (centre - south)
        - jnp.minimum(speed_x, 0.0) * (north - centre)
    )
    result = (
        result
        - jnp.maximum(speed_y, 0.0) * (centre - west)
        - jnp.minimum(speed_y, 0.0) * (east - centre)
    )
    return result + diffusion * (north + south + east + west - 4.0 * centre)


def inverse_root(precision_matrix):
    size_n = precision_matrix.shape[0]
    identity = jnp.eye(size_n, dtype=jnp.float32)
    scale = jnp.trace(precision_matrix)
    start = (precision_matrix / scale, identity)

    def newton_step(index, carry):
        upper, lower = carry
        middle = 1.5 * identity - 0.5 * jnp.dot(
            lower, upper, precision=lax.Precision.HIGHEST, preferred_element_type=jnp.float32
        )
        upper = jnp.dot(
            upper, middle, precision=lax.Precision.HIGHEST, preferred_element_type=jnp.float32
        )
        lower = jnp.dot(
            middle, lower, precision=lax.Precision.HIGHEST, preferred_element_type=jnp.float32
        )
        return (upper, lower)

    upper, lower = lax.fori_loop(0, ROOT_STEPS, newton_step, start)
    return (lower, scale)


def analysis(gram, gain, members):
    identity = jnp.eye(members, dtype=jnp.float32)
    precision_matrix = gram + (members - 1.0) * identity
    root_inverse, scale = inverse_root(precision_matrix)
    half_way = jnp.dot(
        root_inverse, gain, precision=lax.Precision.HIGHEST, preferred_element_type=jnp.float32
    )
    mean_weights = (
        jnp.dot(
            root_inverse,
            half_way,
            precision=lax.Precision.HIGHEST,
            preferred_element_type=jnp.float32,
        )
        / scale
    )
    root = jnp.sqrt((members - 1.0) / scale) * root_inverse
    blend = mean_weights[:, None] + root
    transform = blend - jnp.mean(blend, axis=0, keepdims=True) + 1.0 / members
    return transform.astype(jnp.bfloat16)


def observation_terms(predicted, slot_ids, obs_count, obs_value, obs_var):
    ybar = jnp.mean(predicted, axis=0)
    spread = predicted - ybar[None, :]
    live = (slot_ids < obs_count).astype(jnp.float32)
    weight = live / jnp.sqrt(obs_var)
    scaled = spread * weight[None, :]
    gram_part = jnp.dot(
        scaled, scaled.T, precision=lax.Precision.HIGHEST, preferred_element_type=jnp.float32
    )
    innovation = weight * (obs_value - ybar)
    gain_part = jnp.dot(
        scaled, innovation, precision=lax.Precision.HIGHEST, preferred_element_type=jnp.float32
    )
    return (gram_part, gain_part)


def shards(prior_sample_set, wind_table, regimes, obs_index, obs_count, obs_value, obs_var):
    members_on_device = prior_sample_set.shape[0]
    tile_rows = prior_sample_set.shape[2]
    row_total = tile_rows * lax.axis_size("cell")
    first_row = lax.axis_index("cell") * tile_rows
    sample_set_values = prior_sample_set
    for step in range(SUBSTEPS):
        padded = padded_2(sample_set_values, (("cell", 2),), 1)
        row_ids = first_row + jnp.arange(tile_rows)
        speed_x, speed_y = row_speeds(row_ids, regimes[:, step], wind_table, row_total)
        sample_set_values = stencil(padded, speed_x, speed_y)
    first_cloud_cover = sample_set_values[:, 0].reshape(members_on_device, -1)
    slots_total = obs_index.shape[1]
    cell_hits = (jnp.arange(first_cloud_cover.shape[1])[:, None] == obs_index[0][None, :]).astype(
        jnp.float32
    )
    local_pred = jnp.dot(
        first_cloud_cover,
        cell_hits,
        precision=lax.Precision.HIGHEST,
        preferred_element_type=jnp.float32,
    )
    predicted = lax.all_gather(local_pred, "member", axis=0, tiled=True)
    slot_ids = jnp.arange(slots_total)
    gram_part, gain_part = observation_terms(
        predicted, slot_ids, obs_count[0], obs_value[0], obs_var[0]
    )
    gram, gain = lax.psum((gram_part, gain_part), "cell")
    members = gram.shape[0]
    update_matrix_reduced_precise = analysis(gram, gain, members)
    predicted_reduced_precise = sample_set_values.astype(jnp.bfloat16).reshape(
        members_on_device, prior_sample_set.shape[1], -1
    )
    my_columns = lax.dynamic_slice_in_dim(
        update_matrix_reduced_precise,
        lax.axis_index("member") * members_on_device,
        members_on_device,
        1,
    )
    initial = jnp.zeros(predicted_reduced_precise.shape, jnp.float32)
    piece = lax.all_gather(predicted_reduced_precise, "member", axis=0, tiled=True)
    coeffs = lax.slice_in_dim(my_columns, 0, piece.shape[0], axis=0)
    blended = initial + jnp.einsum("ij,ifc->jfc", coeffs, piece, preferred_element_type=jnp.float32)
    return blended.reshape(prior_sample_set.shape)


def solution(mesh):
    return jax.shard_map(
        shards,
        mesh=mesh,
        in_specs=(
            P(("groups", "member"), None, "cell", None),
            P(),
            P("groups", None),
            P(("groups", "cell"), None),
            P(("groups", "cell")),
            P(("groups", "cell"), None),
            P(("groups", "cell"), None),
        ),
        out_specs=P(("groups", "member"), None, "cell", None),
        check_vma=False,
    )
```

profile of v0, /device:TPU:0, one launch (start us, length us, event | category | flops | bytes accessed | tf_op | source)
XLA Modules:
  0.0 187.4 jit_solution(12085723953323743771)
XLA Ops:
  7.4 3.7 %copy.46 = f32[64,3,8,512]{3,0,2,1:T(8,128)S(1)} copy(f32[64,3,8,512]{3,2,1,0:T(8,128)} %param.9) | data formatting | bytes 6291456 | tf_op args[0]
  11.9 5.7 %collective-permute-start = (f32[64,3,1,512]{3,0,2,1:T(8,128)}, f32[64,3,1,512]{3,0,2,1:T(8,128)}, u32[]{:S(2)}, u32[]{:S(2)}) collective-permute-start(f32[64,3,1,512]{3,0,2,1:T(8,128)} %get-tuple-element.68), channel_id=1, source_target_pairs={{0,4},{4,8},{8,12},{1,5},{5,9},{9,13},{2,6},{6,10},{10,14},{3,7},{... | collective-permute-start | bytes 1179656 | tf_op jit(solution)/shard_map/ppermute | solution.py:20
  21.4 4.1 %collective-permute-done = f32[64,3,1,512]{3,0,2,1:T(8,128)} collective-permute-done((f32[64,3,1,512]{3,0,2,1:T(8,128)}, f32[64,3,1,512]{3,0,2,1:T(8,128)}, u32[]{:S(2)}, u32[]{:S(2)}) %collective-permute-start) | collective-permute-done | bytes 393248 | tf_op jit(solution)/shard_map/ppermute | solution.py:20
  25.5 4.6 %collective-permute-done.1 = f32[64,3,1,512]{3,0,2,1:T(8,128)} collective-permute-done((f32[64,3,1,512]{3,0,2,1:T(8,128)S(1)}, f32[64,3,1,512]{3,0,2,1:T(8,128)}, u32[]{:S(2)}, u32[]{:S(2)}) %collective-permute-start.1) | collective-permute-done | bytes 393248 | tf_op jit(solution)/shard_map/ppermute | solution.py:22
  30.2 4.2 %fusion.53 = f32[64,3,8,512]{3,0,2,1:T(8,128)S(1)} fusion(f32[64,3,1,512]{3,0,2,1:T(8,128)} %collective-permute-done.1, f32[64,3,8,512]{3,0,2,1:T(8,128)S(1)} %copy.46, f32[64,3,1,512]{3,0,2,1:T(8,128)} %collective-permute-done, f32[8]{0:T(128)S(1)} %get-tuple-element.92, f32[8]{0:T(128)S(1)} %get-tuple-element.93, f32[8]{0:T(128)S(1)} %get-tuple-element.91, ...), kind=kLoop, calls=%fused_computation.71 | loop fusion | flops 16515072 | bytes 7078016 | tf_op jit(solution)/shard_map/add | solution.py:60
  34.5 2.8 %collective-permute-start.2 = (f32[64,3,1,512]{3,0,2,1:T(8,128)S(1)}, f32[64,3,1,512]{3,0,2,1:T(8,128)S(1)}, u32[]{:S(2)}, u32[]{:S(2)}) collective-permute-start(f32[64,3,1,512]{3,0,2,1:T(8,128)S(1)} %get-tuple-element.66), channel_id=1, source_target_pairs={{0,4},{4,8},{8,12},{1,5},{5,9},{9,13},{2,6},{6,10},{10,14},{3,7},{... | collective-permute-start | bytes 1179656 | tf_op jit(solution)/shard_map/ppermute | solution.py:20
  38.7 5.7 %collective-permute-done.2 = f32[64,3,1,512]{3,0,2,1:T(8,128)S(1)} collective-permute-done((f32[64,3,1,512]{3,0,2,1:T(8,128)S(1)}, f32[64,3,1,512]{3,0,2,1:T(8,128)S(1)}, u32[]{:S(2)}, u32[]{:S(2)}) %collective-permute-start.2) | collective-permute-done | bytes 393248 | tf_op jit(solution)/shard_map/ppermute | solution.py:20
  44.4 4.1 %collective-permute-done.3 = f32[64,3,1,512]{3,0,2,1:T(8,128)S(1)} collective-permute-done((f32[64,3,1,512]{3,0,2,1:T(8,128)S(1)}, f32[64,3,1,512]{3,0,2,1:T(8,128)S(1)}, u32[]{:S(2)}, u32[]{:S(2)}) %collective-permute-start.3) | collective-permute-done | bytes 393248 | tf_op jit(solution)/shard_map/ppermute | solution.py:22
  48.5 3.1 %fusion.39 = f32[64,3,8,512]{3,0,2,1:T(8,128)S(1)} fusion(f32[64,3,1,512]{3,0,2,1:T(8,128)S(1)} %collective-permute-done.3, f32[64,3,8,512]{3,0,2,1:T(8,128)S(1)} %fusion.53, f32[64,3,1,512]{3,0,2,1:T(8,128)S(1)} %collective-permute-done.2, f32[8]{0:T(128)S(1)} %get-tuple-element.88, f32[8]{0:T(128)S(1)} %get-tuple-element.89, f32[8]{0:T(128)S(1)} %get-tuple-element.87, ...), kind=kLoop, calls=%fused_computation.55 | loop fusion | flops 16515072 | bytes 7078016 | tf_op jit(solution)/shard_map/add | solution.py:60
  51.7 3.5 %collective-permute-start.4 = (f32[64,3,1,512]{3,0,2,1:T(8,128)S(1)}, f32[64,3,1,512]{3,0,2,1:T(8,128)S(1)}, u32[]{:S(2)}, u32[]{:S(2)}) collective-permute-start(f32[64,3,1,512]{3,0,2,1:T(8,128)S(1)} %get-tuple-element.64), channel_id=1, source_target_pairs={{0,4},{4,8},{8,12},{1,5},{5,9},{9,13},{2,6},{6,10},{10,14},{3,7},{... | collective-permute-start | bytes 1179656 | tf_op jit(solution)/shard_map/ppermute | solution.py:20
  56.7 4.4 %collective-permute-done.4 = f32[64,3,1,512]{3,0,2,1:T(8,128)S(1)} collective-permute-done((f32[64,3,1,512]{3,0,2,1:T(8,128)S(1)}, f32[64,3,1,512]{3,0,2,1:T(8,128)S(1)}, u32[]{:S(2)}, u32[]{:S(2)}) %collective-permute-start.4) | collective-permute-done | bytes 393248 | tf_op jit(solution)/shard_map/ppermute | solution.py:20
  61.1 4.1 %collective-permute-done.5 = f32[64,3,1,512]{3,0,2,1:T(8,128)S(1)} collective-permute-done((f32[64,3,1,512]{3,0,2,1:T(8,128)S(1)}, f32[64,3,1,512]{3,0,2,1:T(8,128)S(1)}, u32[]{:S(2)}, u32[]{:S(2)}) %collective-permute-start.5) | collective-permute-done | bytes 393248 | tf_op jit(solution)/shard_map/ppermute | solution.py:22
  65.3 3.2 %fusion.25 = f32[64,3,8,512]{3,0,2,1:T(8,128)S(1)} fusion(f32[64,3,1,512]{3,0,2,1:T(8,128)S(1)} %collective-permute-done.5, f32[64,3,8,512]{3,0,2,1:T(8,128)S(1)} %fusion.39, f32[64,3,1,512]{3,0,2,1:T(8,128)S(1)} %collective-permute-done.4, f32[8]{0:T(128)S(1)} %get-tuple-element.84, f32[8]{0:T(128)S(1)} %get-tuple-element.85, f32[8]{0:T(128)S(1)} %get-tuple-element.83, ...), kind=kLoop, calls=%fused_computation.39 | loop fusion | flops 16515072 | bytes 7078016 | tf_op jit(solution)/shard_map/add | solution.py:60
  68.5 2.5 %collective-permute-start.6 = (f32[64,3,1,512]{3,0,2,1:T(8,128)S(1)}, f32[64,3,1,512]{3,0,2,1:T(8,128)S(1)}, u32[]{:S(2)}, u32[]{:S(2)}) collective-permute-start(f32[64,3,1,512]{3,0,2,1:T(8,128)S(1)} %get-tuple-element.62), channel_id=1, source_target_pairs={{0,4},{4,8},{8,12},{1,5},{5,9},{9,13},{2,6},{6,10},{10,14},{3,7},{... | collective-permute-start | bytes 1179656 | tf_op jit(solution)/shard_map/ppermute | solution.py:20
  72.4 3.9 %collective-permute-done.6 = f32[64,3,1,512]{3,0,2,1:T(8,128)S(1)} collective-permute-done((f32[64,3,1,512]{3,0,2,1:T(8,128)S(1)}, f32[64,3,1,512]{3,0,2,1:T(8,128)S(1)}, u32[]{:S(2)}, u32[]{:S(2)}) %collective-permute-start.6) | collective-permute-done | bytes 393248 | tf_op jit(solution)/shard_map/ppermute | solution.py:20
  76.3 4.4 %collective-permute-done.7 = f32[64,3,1,512]{3,0,2,1:T(8,128)S(1)} collective-permute-done((f32[64,3,1,512]{3,0,2,1:T(8,128)S(1)}, f32[64,3,1,512]{3,0,2,1:T(8,128)S(1)}, u32[]{:S(2)}, u32[]{:S(2)}) %collective-permute-start.7) | collective-permute-done | bytes 393248 | tf_op jit(solution)/shard_map/ppermute | solution.py:22
  80.7 3.4 %convert_bitcast_fusion = (bf16[3,8,8,8,512]{4,3,2,1,0:T(8,128)(2,1)S(1)}, f32[64,3,8,512]{3,0,2,1:T(8,128)S(1)}) fusion(f32[64,3,8,512]{3,0,2,1:T(8,128)S(1)} %fusion.25, f32[8]{0:T(128)S(1)} %get-tuple-element.80, f32[8]{0:T(128)S(1)} %get-tuple-element.81, f32[64,3,1,512]{3,0,2,1:T(8,128)S(1)} %collective-permute-done.7, f32[8]{0:T(128)S(1)} %get-tuple-element.79, ...), kind=kLoop, calls=%fused_computation.80 | loop fusion | flops 17301504 | bytes 8650880
  84.7 3.0 %fusion.3 = f32[64,512]{1,0:T(8,128)S(1)} fusion(f32[64,4096]{1,0:T(8,128)S(1)} %bitcast.108, s32[512]{0:T(512)S(1)} %bitcast.117), kind=kOutput, calls=%fused_computation.6 | convolution fusion | flops 1612709888 | bytes 1181696 | tf_op jit(solution)/shard_map/dot_general | solution.py:140
  87.8 7.4 %all_gather.6 = f32[256,512]{1,0:T(8,128)S(1)} all-gather(f32[64,512]{1,0:T(8,128)S(1)} %fusion.3), channel_id=1, replica_groups=mesh['groups'=2,'cell'=4,'member'=4] {'member'}, dimensions={0}, use_global_device_ids=true | all-gather | bytes 655360 | tf_op jit(solution)/shard_map/all_gather | solution.py:146
  98.5 8.6 %psum.15 = f32[256]{0:T(256)S(1)} all-reduce(f32[256]{0:T(256)S(1)} %bitcast.114), channel_id=1, replica_groups=mesh['groups'=2,'cell'=4,'member'=4] {'cell'}, use_global_device_ids=true, to_apply=%region_9.10 | all-reduce | flops 256 | bytes 2048 | tf_op jit(solution)/shard_map/psum | solution.py:151
  107.2 22.7 %all-reduce.6.cloned.1.call-done = f32[256,256]{1,0:T(8,128)} async-done(((f32[256,256]{1,0:T(8,128)}), f32[256,256]{1,0:T(8,128)}) %all-reduce.6.cloned.1.call-update) | async-done | bytes 262160 | tf_op jit(solution)/shard_map/psum | solution.py:151
  133.4 35.4 %while.13 = (s32[]{:T(128)}, f32[256,256]{0,1:T(8,128)S(1)}, f32[256,256]{1,0:T(8,128)S(1)}, s32[]{:T(128)}) while((s32[]{:T(128)}, f32[256,256]{0,1:T(8,128)S(1)}, f32[256,256]{1,0:T(8,128)S(1)}, s32[]{:T(128)}) %tuple.51), condition=%wide.region_8.9_spmd.clone, body=%wide.region_7.8_spmd.clone.sunk | while | flops 604241920 | bytes 3407925 | solution.py:82
  171.2 4.0 %fusion.72 = f32[64,3,4096]{2,0,1:T(8,128)S(1)} fusion(bf16[256,3,4096]{2,0,1:T(8,128)(2,1)} %all-gather.2.cloned.1.call-done, f32[256,256]{0,1:T(8,128)S(1)} %get-tuple-element.59, s32[]{:T(128)S(6)} %select_n.22, f32[64]{0:T(128)S(1)} %dynamic-slice), kind=kOutput, calls=%fused_computation.99 | convolution fusion | flops 402702336 | bytes 9503236 | tf_op jit(solution)/shard_map/ij,ifc->jfc/dot_general | solution.py:166
  175.3 2.7 %copy.61 = f32[24,8,8,512]{3,2,1,0:T(8,128)S(1)} copy(f32[24,8,8,512]{3,1,2,0:T(8,128)S(1)} %bitcast.105) | data formatting | bytes 6291456
  (174 shorter events, 53.6 us)
Async XLA Ops:
  7.4 13.7 %copy-start = (f32[8,2]{0,1:T(2,128)S(1)}, f32[8,2]{0,1:T(2,128)}, u32[]{:S(2)}) copy-start(f32[8,2]{0,1:T(2,128)} %param.10) | copy-start | bytes 196
  7.4 11.5 %copy-start.1 = (s32[8,4]{0,1:T(4,128)S(1)}, s32[8,4]{0,1:T(4,128)}, u32[]{:S(2)}) copy-start(s32[8,4]{0,1:T(4,128)} %param.11) | copy-start | bytes 388
  7.4 122.5 %all-reduce.6.cloned.1.call-start = ((), (), s32[]{:S(2)}) async-start(), calls=%async_computation | async-start | bytes 524288 | tf_op jit(solution)/shard_map/psum | solution.py:151
  11.9 13.6 %collective-permute-start = (f32[64,3,1,512]{3,0,2,1:T(8,128)}, f32[64,3,1,512]{3,0,2,1:T(8,128)}, u32[]{:S(2)}, u32[]{:S(2)}) collective-permute-start(f32[64,3,1,512]{3,0,2,1:T(8,128)} %get-tuple-element.68), channel_id=1, source_target_pairs={{0,4},{4,8},{8,12},{1,5},{5,9},{9,13},{2,6},{6,10},{10,14},{3,7},{... | collective-permute-start | bytes 1179656 | tf_op jit(solution)/shard_map/ppermute | solution.py:20
  17.6 12.6 %collective-permute-start.1 = (f32[64,3,1,512]{3,0,2,1:T(8,128)S(1)}, f32[64,3,1,512]{3,0,2,1:T(8,128)}, u32[]{:S(2)}, u32[]{:S(2)}) collective-permute-start(f32[64,3,1,512]{3,0,2,1:T(8,128)S(1)} %get-tuple-element.69), channel_id=1, source_target_pairs={{4,0},{8,4},{12,8},{5,1},{9,5},{13,9},{6,2},{10,6},{14,10},{7,3},{... | collective-permute-start | bytes 1179656 | tf_op jit(solution)/shard_map/ppermute | solution.py:22
  34.5 9.9 %collective-permute-start.2 = (f32[64,3,1,512]{3,0,2,1:T(8,128)S(1)}, f32[64,3,1,512]{3,0,2,1:T(8,128)S(1)}, u32[]{:S(2)}, u32[]{:S(2)}) collective-permute-start(f32[64,3,1,512]{3,0,2,1:T(8,128)S(1)} %get-tuple-element.66), channel_id=1, source_target_pairs={{0,4},{4,8},{8,12},{1,5},{5,9},{9,13},{2,6},{6,10},{10,14},{3,7},{... | collective-permute-start | bytes 1179656 | tf_op jit(solution)/shard_map/ppermute | solution.py:20
  37.2 11.3 %collective-permute-start.3 = (f32[64,3,1,512]{3,0,2,1:T(8,128)S(1)}, f32[64,3,1,512]{3,0,2,1:T(8,128)S(1)}, u32[]{:S(2)}, u32[]{:S(2)}) collective-permute-start(f32[64,3,1,512]{3,0,2,1:T(8,128)S(1)} %get-tuple-element.67), channel_id=1, source_target_pairs={{4,0},{8,4},{12,8},{5,1},{9,5},{13,9},{6,2},{10,6},{14,10},{7,3},{... | collective-permute-start | bytes 1179656 | tf_op jit(solution)/shard_map/ppermute | solution.py:22
  51.7 9.4 %collective-permute-start.4 = (f32[64,3,1,512]{3,0,2,1:T(8,128)S(1)}, f32[64,3,1,512]{3,0,2,1:T(8,128)S(1)}, u32[]{:S(2)}, u32[]{:S(2)}) collective-permute-start(f32[64,3,1,512]{3,0,2,1:T(8,128)S(1)} %get-tuple-element.64), channel_id=1, source_target_pairs={{0,4},{4,8},{8,12},{1,5},{5,9},{9,13},{2,6},{6,10},{10,14},{3,7},{... | collective-permute-start | bytes 1179656 | tf_op jit(solution)/shard_map/ppermute | solution.py:20
  55.2 10.1 %collective-permute-start.5 = (f32[64,3,1,512]{3,0,2,1:T(8,128)S(1)}, f32[64,3,1,512]{3,0,2,1:T(8,128)S(1)}, u32[]{:S(2)}, u32[]{:S(2)}) collective-permute-start(f32[64,3,1,512]{3,0,2,1:T(8,128)S(1)} %get-tuple-element.65), channel_id=1, source_target_pairs={{4,0},{8,4},{12,8},{5,1},{9,5},{13,9},{6,2},{10,6},{14,10},{7,3},{... | collective-permute-start | bytes 1179656 | tf_op jit(solution)/shard_map/ppermute | solution.py:22
  65.3 7.1 %copy-start.2 = (f32[1,512]{1,0:T(1,128)S(1)}, f32[1,512]{1,0:T(1,128)}, u32[]{:S(2)}) copy-start(f32[1,512]{1,0:T(1,128)} %param.15) | copy-start | bytes 6148
  68.5 7.7 %collective-permute-start.6 = (f32[64,3,1,512]{3,0,2,1:T(8,128)S(1)}, f32[64,3,1,512]{3,0,2,1:T(8,128)S(1)}, u32[]{:S(2)}, u32[]{:S(2)}) collective-permute-start(f32[64,3,1,512]{3,0,2,1:T(8,128)S(1)} %get-tuple-element.62), channel_id=1, source_target_pairs={{0,4},{4,8},{8,12},{1,5},{5,9},{9,13},{2,6},{6,10},{10,14},{3,7},{... | collective-permute-start | bytes 1179656 | tf_op jit(solution)/shard_map/ppermute | solution.py:20
  71.0 9.7 %collective-permute-start.7 = (f32[64,3,1,512]{3,0,2,1:T(8,128)S(1)}, f32[64,3,1,512]{3,0,2,1:T(8,128)S(1)}, u32[]{:S(2)}, u32[]{:S(2)}) collective-permute-start(f32[64,3,1,512]{3,0,2,1:T(8,128)S(1)} %get-tuple-element.63), channel_id=1, source_target_pairs={{4,0},{8,4},{12,8},{5,1},{9,5},{13,9},{6,2},{10,6},{14,10},{7,3},{... | collective-permute-start | bytes 1179656 | tf_op jit(solution)/shard_map/ppermute | solution.py:22
  84.1 0.7 copy-start.4
  84.1 11.1 %copy-start.3 = (f32[1,512]{1,0:T(1,128)S(1)}, f32[1,512]{1,0:T(1,128)}, u32[]{:S(2)}) copy-start(f32[1,512]{1,0:T(1,128)} %param.14) | copy-start | bytes 6148
  96.6 74.6 %all-gather.2.cloned.1.call-start = ((), (), s32[]{:S(2)}) async-start(), calls=%async_computation.1 | async-start | bytes 7864320 | tf_op jit(solution)/shard_map/all_gather | solution.py:164
Sparse Core Ops, SparseCore 0:
  96.7 33.1 all-reduce.5
Sparse Core Ops, SparseCore 1:
  107.3 44.9 all-gather.1
where the time goes:
time: 188 us; the launch traced here: 187 us
  waiting for transfers between devices  58.2 us (31%)
  matrix products  43.5 us (23%)
  starting transfers between devices  19.6 us (10%)
  other arithmetic  19.1 us (10%)
  between operations  16.5 us (9%)
  blocking collectives  16 us (9%)
  local copies, waits for them, and re-layouts  13.2 us (7%)
    psum x1, waiting for transfers between devices, shards(): gram, gain = lax.psum((gram_part, gain_part), 'cell')  22.7 us
    ppermute x4, waiting for transfers between devices, padded_2(): lax.ppermute(tail, axis, [(i, (i + 1) % count) for i in range(ends)])  18.1 us
    ppermute x4, waiting for transfers between devices, padded_2(): lax.ppermute(head, axis, [((i + 1) % count, i) for i in range(ends)])  17.3 us
    ppermute x4, starting transfers between devices, padded_2(): lax.ppermute(tail, axis, [(i, (i + 1) % count) for i in range(ends)])  14.4 us
    dot_general x24, matrix products, newton_step(): jnp.dot(upper, middle, precision=lax.Precision.HIGHEST, preferred_element...  14.3 us
    add x3, other arithmetic, stencil(): return result + diffusion * (north + south + east + west - 4.0 * centre)  10.5 us
    dot_general x24, matrix products, newton_step(): jnp.dot(lower, upper, precision=lax.Precision.HIGHEST, preferred_element_...  9.83 us
    dot_general x24, matrix products, newton_step(): jnp.dot(middle, lower, precision=lax.Precision.HIGHEST, preferred_element...  9.07 us
  transfers between devices with their start and end apart: 10, of which 9 were waited for; matrix products, arithmetic and copies ran while one was open for 23% of the time, Pallas kernels for 0%

commit v1 on v0

--- a/solution.py
+++ b/solution.py
@@ -143,7 +143,14 @@
         precision=lax.Precision.HIGHEST,
         preferred_element_type=jnp.float32,
     )
-    predicted = lax.all_gather(local_pred, "member", axis=0, tiled=True)
+    ring = [local_pred]
+    for hop in range(3):
+        ring.append(lax.ppermute(ring[-1], "member", [(dev, (dev + 1) % 4) for dev in range(4)]))
+    predicted = jnp.roll(
+        jnp.concatenate(ring[::-1], axis=0),
+        (lax.axis_index("member") + 1) * ring[0].shape[0],
+        axis=0,
+    )
     slot_ids = jnp.arange(slots_total)
     gram_part, gain_part = observation_terms(
         predicted, slot_ids, obs_count[0], obs_value[0], obs_var[0]

time: 188 us -> 194 us (1.032)
  waiting for transfers between devices: 58.2 us -> 71.8 us
  blocking collectives: 16 us -> 8.65 us
    ppermute x0 -> x3, waiting for transfers between devices: none -> 12.5 us  [shards(): lax.ppermute(ring[-1], 'member', [(dev, (dev + 1) % 4) for dev in range(4)])]
    all_gather x1 -> x0, blocking collectives: 7.35 us -> none  [shards(): predicted = lax.all_gather(local_pred, 'member', axis=0, tiled=True)]
    unnamed x15 -> x22, local copies, waits for them, and re-layouts: 7.25 us -> 7.32 us
  transfers between devices with their start and end apart: 10 -> 13, of which waited for: 9 -> 12; matrix products, arithmetic and copies ran while one was open for 23% -> 22% of each run, Pallas kernels for 0% -> 0%
where the time goes in v1:
time: 194 us
  waiting for transfers between devices  71.8 us (37%)
  matrix products  43.5 us (22%)
  starting transfers between devices  19.7 us (10%)
  other arithmetic  19.1 us (10%)
  between operations  16.6 us (9%)
  local copies, waits for them, and re-layouts  13.3 us (7%)
  blocking collectives  8.65 us (4%)
    psum x1, waiting for transfers between devices, shards(): gram, gain = lax.psum((gram_part, gain_part), 'cell')  23.2 us
    ppermute x4, waiting for transfers between devices, padded_2(): lax.ppermute(tail, axis, [(i, (i + 1) % count) for i in range(ends)])  18.8 us
    ppermute x4, waiting for transfers between devices, padded_2(): lax.ppermute(head, axis, [((i + 1) % count, i) for i in range(ends)])  17.3 us
    ppermute x4, starting transfers between devices, padded_2(): lax.ppermute(tail, axis, [(i, (i + 1) % count) for i in range(ends)])  14.4 us
    dot_general x24, matrix products, newton_step(): jnp.dot(upper, middle, precision=lax.Precision.HIGHEST, preferred_element...  14.3 us
    ppermute x3, waiting for transfers between devices, shards(): lax.ppermute(ring[-1], 'member', [(dev, (dev + 1) % 4) for dev in range(4)])  12.5 us
    add x3, other arithmetic, stencil(): return result + diffusion * (north + south + east + west - 4.0 * centre)  10.5 us
    dot_general x24, matrix products, newton_step(): jnp.dot(lower, upper, precision=lax.Precision.HIGHEST, preferred_element_...  9.83 us
  transfers between devices with their start and end apart: 13, of which 12 were waited for; matrix products, arithmetic and copies ran while one was open for 22% of the time, Pallas kernels for 0%

profile of v1, /device:TPU:0, one launch (start us, length us, event | category | flops | bytes accessed | tf_op | source)
XLA Modules:
  0.0 194.0 jit_solution(14428742364471341344)
XLA Ops:
  7.4 3.7 %copy.46 = f32[64,3,8,512]{3,0,2,1:T(8,128)S(1)} copy(f32[64,3,8,512]{3,2,1,0:T(8,128)} %param.9) | data formatting | bytes 6291456 | tf_op args[0]
  11.9 5.7 %collective-permute-start = (f32[64,3,1,512]{3,0,2,1:T(8,128)}, f32[64,3,1,512]{3,0,2,1:T(8,128)}, u32[]{:S(2)}, u32[]{:S(2)}) collective-permute-start(f32[64,3,1,512]{3,0,2,1:T(8,128)} %get-tuple-element.68), channel_id=1, source_target_pairs={{0,4},{4,8},{8,12},{1,5},{5,9},{9,13},{2,6},{6,10},{10,14},{3,7},{... | collective-permute-start | bytes 1179656 | tf_op jit(solution)/shard_map/ppermute | solution.py:20
  20.6 4.9 %collective-permute-done = f32[64,3,1,512]{3,0,2,1:T(8,128)} collective-permute-done((f32[64,3,1,512]{3,0,2,1:T(8,128)}, f32[64,3,1,512]{3,0,2,1:T(8,128)}, u32[]{:S(2)}, u32[]{:S(2)}) %collective-permute-start) | collective-permute-done | bytes 393248 | tf_op jit(solution)/shard_map/ppermute | solution.py:20
  25.5 4.6 %collective-permute-done.1 = f32[64,3,1,512]{3,0,2,1:T(8,128)} collective-permute-done((f32[64,3,1,512]{3,0,2,1:T(8,128)S(1)}, f32[64,3,1,512]{3,0,2,1:T(8,128)}, u32[]{:S(2)}, u32[]{:S(2)}) %collective-permute-start.1) | collective-permute-done | bytes 393248 | tf_op jit(solution)/shard_map/ppermute | solution.py:22
  30.2 4.2 %fusion.53 = f32[64,3,8,512]{3,0,2,1:T(8,128)S(1)} fusion(f32[64,3,1,512]{3,0,2,1:T(8,128)} %collective-permute-done.1, f32[64,3,8,512]{3,0,2,1:T(8,128)S(1)} %copy.46, f32[64,3,1,512]{3,0,2,1:T(8,128)} %collective-permute-done, f32[8]{0:T(128)S(1)} %get-tuple-element.92, f32[8]{0:T(128)S(1)} %get-tuple-element.93, f32[8]{0:T(128)S(1)} %get-tuple-element.91, ...), kind=kLoop, calls=%fused_computation.71 | loop fusion | flops 16515072 | bytes 7078016 | tf_op jit(solution)/shard_map/add | solution.py:60
  34.4 2.8 %collective-permute-start.2 = (f32[64,3,1,512]{3,0,2,1:T(8,128)S(1)}, f32[64,3,1,512]{3,0,2,1:T(8,128)S(1)}, u32[]{:S(2)}, u32[]{:S(2)}) collective-permute-start(f32[64,3,1,512]{3,0,2,1:T(8,128)S(1)} %get-tuple-element.66), channel_id=1, source_target_pairs={{0,4},{4,8},{8,12},{1,5},{5,9},{9,13},{2,6},{6,10},{10,14},{3,7},{... | collective-permute-start | bytes 1179656 | tf_op jit(solution)/shard_map/ppermute | solution.py:20
  38.7 5.6 %collective-permute-done.2 = f32[64,3,1,512]{3,0,2,1:T(8,128)S(1)} collective-permute-done((f32[64,3,1,512]{3,0,2,1:T(8,128)S(1)}, f32[64,3,1,512]{3,0,2,1:T(8,128)S(1)}, u32[]{:S(2)}, u32[]{:S(2)}) %collective-permute-start.2) | collective-permute-done | bytes 393248 | tf_op jit(solution)/shard_map/ppermute | solution.py:20
  44.4 4.1 %collective-permute-done.3 = f32[64,3,1,512]{3,0,2,1:T(8,128)S(1)} collective-permute-done((f32[64,3,1,512]{3,0,2,1:T(8,128)S(1)}, f32[64,3,1,512]{3,0,2,1:T(8,128)S(1)}, u32[]{:S(2)}, u32[]{:S(2)}) %collective-permute-start.3) | collective-permute-done | bytes 393248 | tf_op jit(solution)/shard_map/ppermute | solution.py:22
  48.5 3.1 %fusion.39 = f32[64,3,8,512]{3,0,2,1:T(8,128)S(1)} fusion(f32[64,3,1,512]{3,0,2,1:T(8,128)S(1)} %collective-permute-done.3, f32[64,3,8,512]{3,0,2,1:T(8,128)S(1)} %fusion.53, f32[64,3,1,512]{3,0,2,1:T(8,128)S(1)} %collective-permute-done.2, f32[8]{0:T(128)S(1)} %get-tuple-element.88, f32[8]{0:T(128)S(1)} %get-tuple-element.89, f32[8]{0:T(128)S(1)} %get-tuple-element.87, ...), kind=kLoop, calls=%fused_computation.55 | loop fusion | flops 16515072 | bytes 7078016 | tf_op jit(solution)/shard_map/add | solution.py:60
  51.7 3.5 %collective-permute-start.4 = (f32[64,3,1,512]{3,0,2,1:T(8,128)S(1)}, f32[64,3,1,512]{3,0,2,1:T(8,128)S(1)}, u32[]{:S(2)}, u32[]{:S(2)}) collective-permute-start(f32[64,3,1,512]{3,0,2,1:T(8,128)S(1)} %get-tuple-element.64), channel_id=1, source_target_pairs={{0,4},{4,8},{8,12},{1,5},{5,9},{9,13},{2,6},{6,10},{10,14},{3,7},{... | collective-permute-start | bytes 1179656 | tf_op jit(solution)/shard_map/ppermute | solution.py:20
  56.7 4.4 %collective-permute-done.4 = f32[64,3,1,512]{3,0,2,1:T(8,128)S(1)} collective-permute-done((f32[64,3,1,512]{3,0,2,1:T(8,128)S(1)}, f32[64,3,1,512]{3,0,2,1:T(8,128)S(1)}, u32[]{:S(2)}, u32[]{:S(2)}) %collective-permute-start.4) | collective-permute-done | bytes 393248 | tf_op jit(solution)/shard_map/ppermute | solution.py:20
  61.1 4.1 %collective-permute-done.5 = f32[64,3,1,512]{3,0,2,1:T(8,128)S(1)} collective-permute-done((f32[64,3,1,512]{3,0,2,1:T(8,128)S(1)}, f32[64,3,1,512]{3,0,2,1:T(8,128)S(1)}, u32[]{:S(2)}, u32[]{:S(2)}) %collective-permute-start.5) | collective-permute-done | bytes 393248 | tf_op jit(solution)/shard_map/ppermute | solution.py:22
  65.3 3.2 %fusion.25 = f32[64,3,8,512]{3,0,2,1:T(8,128)S(1)} fusion(f32[64,3,1,512]{3,0,2,1:T(8,128)S(1)} %collective-permute-done.5, f32[64,3,8,512]{3,0,2,1:T(8,128)S(1)} %fusion.39, f32[64,3,1,512]{3,0,2,1:T(8,128)S(1)} %collective-permute-done.4, f32[8]{0:T(128)S(1)} %get-tuple-element.84, f32[8]{0:T(128)S(1)} %get-tuple-element.85, f32[8]{0:T(128)S(1)} %get-tuple-element.83, ...), kind=kLoop, calls=%fused_computation.39 | loop fusion | flops 16515072 | bytes 7078016 | tf_op jit(solution)/shard_map/add | solution.py:60
  72.5 3.8 %collective-permute-done.6 = f32[64,3,1,512]{3,0,2,1:T(8,128)S(1)} collective-permute-done((f32[64,3,1,512]{3,0,2,1:T(8,128)S(1)}, f32[64,3,1,512]{3,0,2,1:T(8,128)S(1)}, u32[]{:S(2)}, u32[]{:S(2)}) %collective-permute-start.6) | collective-permute-done | bytes 393248 | tf_op jit(solution)/shard_map/ppermute | solution.py:20
  76.3 4.4 %collective-permute-done.7 = f32[64,3,1,512]{3,0,2,1:T(8,128)S(1)} collective-permute-done((f32[64,3,1,512]{3,0,2,1:T(8,128)S(1)}, f32[64,3,1,512]{3,0,2,1:T(8,128)S(1)}, u32[]{:S(2)}, u32[]{:S(2)}) %collective-permute-start.7) | collective-permute-done | bytes 393248 | tf_op jit(solution)/shard_map/ppermute | solution.py:22
  80.7 3.4 %convert_bitcast_fusion = (bf16[3,8,8,8,512]{4,3,2,1,0:T(8,128)(2,1)S(1)}, f32[64,3,8,512]{3,0,2,1:T(8,128)S(1)}) fusion(f32[64,3,8,512]{3,0,2,1:T(8,128)S(1)} %fusion.25, f32[8]{0:T(128)S(1)} %get-tuple-element.80, f32[8]{0:T(128)S(1)} %get-tuple-element.81, f32[64,3,1,512]{3,0,2,1:T(8,128)S(1)} %collective-permute-done.7, f32[8]{0:T(128)S(1)} %get-tuple-element.79, ...), kind=kLoop, calls=%fused_computation.80 | loop fusion | flops 17301504 | bytes 8650880
  84.7 3.0 %fusion.3 = f32[64,512]{1,0:T(8,128)S(1)} fusion(f32[64,4096]{1,0:T(8,128)S(1)} %bitcast.108, s32[512]{0:T(512)S(1)} %bitcast.117), kind=kOutput, calls=%fused_computation.6 | convolution fusion | flops 1612709888 | bytes 1181696 | tf_op jit(solution)/shard_map/dot_general | solution.py:140
  87.9 4.4 %collective-permute-done.8 = f32[64,512]{1,0:T(8,128)S(1)} collective-permute-done((f32[64,512]{1,0:T(8,128)S(1)}, f32[64,512]{1,0:T(8,128)S(1)}, u32[]{:S(2)}, u32[]{:S(2)}) %collective-permute-start.8) | collective-permute-done | bytes 131104 | tf_op jit(solution)/shard_map/ppermute | solution.py:148
  92.9 3.7 %collective-permute-done.9 = f32[64,512]{1,0:T(8,128)S(1)} collective-permute-done((f32[64,512]{1,0:T(8,128)S(1)}, f32[64,512]{1,0:T(8,128)S(1)}, u32[]{:S(2)}, u32[]{:S(2)}) %collective-permute-start.9) | collective-permute-done | bytes 131104 | tf_op jit(solution)/shard_map/ppermute | solution.py:148
  96.6 4.4 %collective-permute-done.10 = f32[64,512]{1,0:T(8,128)S(1)} collective-permute-done((f32[64,512]{1,0:T(8,128)S(1)}, f32[64,512]{1,0:T(8,128)S(1)}, u32[]{:S(2)}, u32[]{:S(2)}) %collective-permute-start.10) | collective-permute-done | bytes 131104 | tf_op jit(solution)/shard_map/ppermute | solution.py:148
  104.6 8.7 %psum.15 = f32[256]{0:T(256)S(1)} all-reduce(f32[256]{0:T(256)S(1)} %bitcast.114), channel_id=1, replica_groups=mesh['groups'=2,'cell'=4,'member'=4] {'cell'}, use_global_device_ids=true, to_apply=%region_9.10 | all-reduce | flops 256 | bytes 2048 | tf_op jit(solution)/shard_map/psum | solution.py:158
  113.3 23.2 %all-reduce.6.cloned.1.call-done = f32[256,256]{1,0:T(8,128)} async-done(((f32[256,256]{1,0:T(8,128)}), f32[256,256]{1,0:T(8,128)}) %all-reduce.6.cloned.1.call-update) | async-done | bytes 262160 | tf_op jit(solution)/shard_map/psum | solution.py:158
  139.9 35.4 %while.13 = (s32[]{:T(128)}, f32[256,256]{0,1:T(8,128)S(1)}, f32[256,256]{1,0:T(8,128)S(1)}, s32[]{:T(128)}) while((s32[]{:T(128)}, f32[256,256]{0,1:T(8,128)S(1)}, f32[256,256]{1,0:T(8,128)S(1)}, s32[]{:T(128)}) %tuple.51), condition=%wide.region_8.9_spmd.clone, body=%wide.region_7.8_spmd.clone.sunk | while | flops 604241920 | bytes 3407925 | solution.py:82
  177.8 4.0 %fusion.72 = f32[64,3,4096]{2,0,1:T(8,128)S(1)} fusion(bf16[256,3,4096]{2,0,1:T(8,128)(2,1)} %all-gather.2.cloned.1.call-done, f32[256,256]{0,1:T(8,128)S(1)} %get-tuple-element.59, s32[]{:T(128)S(6)} %select_n.37, f32[64]{0:T(128)S(1)} %dynamic-slice), kind=kOutput, calls=%fused_computation.100 | convolution fusion | flops 402702336 | bytes 9503236 | tf_op jit(solution)/shard_map/ij,ifc->jfc/dot_general | solution.py:173
  (187 shorter events, 59.0 us)
Async XLA Ops:
  7.4 13.0 %copy-start = (f32[8,2]{0,1:T(2,128)S(1)}, f32[8,2]{0,1:T(2,128)}, u32[]{:S(2)}) copy-start(f32[8,2]{0,1:T(2,128)} %param.10) | copy-start | bytes 196
  7.4 11.5 %copy-start.1 = (s32[8,4]{0,1:T(4,128)S(1)}, s32[8,4]{0,1:T(4,128)}, u32[]{:S(2)}) copy-start(s32[8,4]{0,1:T(4,128)} %param.11) | copy-start | bytes 388
  7.4 129.1 %all-reduce.6.cloned.1.call-start = ((), (), s32[]{:S(2)}) async-start(), calls=%async_computation | async-start | bytes 524288 | tf_op jit(solution)/shard_map/psum | solution.py:158
  11.9 13.6 %collective-permute-start = (f32[64,3,1,512]{3,0,2,1:T(8,128)}, f32[64,3,1,512]{3,0,2,1:T(8,128)}, u32[]{:S(2)}, u32[]{:S(2)}) collective-permute-start(f32[64,3,1,512]{3,0,2,1:T(8,128)} %get-tuple-element.68), channel_id=1, source_target_pairs={{0,4},{4,8},{8,12},{1,5},{5,9},{9,13},{2,6},{6,10},{10,14},{3,7},{... | collective-permute-start | bytes 1179656 | tf_op jit(solution)/shard_map/ppermute | solution.py:20
  17.6 12.6 %collective-permute-start.1 = (f32[64,3,1,512]{3,0,2,1:T(8,128)S(1)}, f32[64,3,1,512]{3,0,2,1:T(8,128)}, u32[]{:S(2)}, u32[]{:S(2)}) collective-permute-start(f32[64,3,1,512]{3,0,2,1:T(8,128)S(1)} %get-tuple-element.69), channel_id=1, source_target_pairs={{4,0},{8,4},{12,8},{5,1},{9,5},{13,9},{6,2},{10,6},{14,10},{7,3},{... | collective-permute-start | bytes 1179656 | tf_op jit(solution)/shard_map/ppermute | solution.py:22
  34.4 9.9 %collective-permute-start.2 = (f32[64,3,1,512]{3,0,2,1:T(8,128)S(1)}, f32[64,3,1,512]{3,0,2,1:T(8,128)S(1)}, u32[]{:S(2)}, u32[]{:S(2)}) collective-permute-start(f32[64,3,1,512]{3,0,2,1:T(8,128)S(1)} %get-tuple-element.66), channel_id=1, source_target_pairs={{0,4},{4,8},{8,12},{1,5},{5,9},{9,13},{2,6},{6,10},{10,14},{3,7},{... | collective-permute-start | bytes 1179656 | tf_op jit(solution)/shard_map/ppermute | solution.py:20
  37.2 11.3 %collective-permute-start.3 = (f32[64,3,1,512]{3,0,2,1:T(8,128)S(1)}, f32[64,3,1,512]{3,0,2,1:T(8,128)S(1)}, u32[]{:S(2)}, u32[]{:S(2)}) collective-permute-start(f32[64,3,1,512]{3,0,2,1:T(8,128)S(1)} %get-tuple-element.67), channel_id=1, source_target_pairs={{4,0},{8,4},{12,8},{5,1},{9,5},{13,9},{6,2},{10,6},{14,10},{7,3},{... | collective-permute-start | bytes 1179656 | tf_op jit(solution)/shard_map/ppermute | solution.py:22
  51.7 9.4 %collective-permute-start.4 = (f32[64,3,1,512]{3,0,2,1:T(8,128)S(1)}, f32[64,3,1,512]{3,0,2,1:T(8,128)S(1)}, u32[]{:S(2)}, u32[]{:S(2)}) collective-permute-start(f32[64,3,1,512]{3,0,2,1:T(8,128)S(1)} %get-tuple-element.64), channel_id=1, source_target_pairs={{0,4},{4,8},{8,12},{1,5},{5,9},{9,13},{2,6},{6,10},{10,14},{3,7},{... | collective-permute-start | bytes 1179656 | tf_op jit(solution)/shard_map/ppermute | solution.py:20
  55.2 10.1 %collective-permute-start.5 = (f32[64,3,1,512]{3,0,2,1:T(8,128)S(1)}, f32[64,3,1,512]{3,0,2,1:T(8,128)S(1)}, u32[]{:S(2)}, u32[]{:S(2)}) collective-permute-start(f32[64,3,1,512]{3,0,2,1:T(8,128)S(1)} %get-tuple-element.65), channel_id=1, source_target_pairs={{4,0},{8,4},{12,8},{5,1},{9,5},{13,9},{6,2},{10,6},{14,10},{7,3},{... | collective-permute-start | bytes 1179656 | tf_op jit(solution)/shard_map/ppermute | solution.py:22
  68.5 7.7 %collective-permute-start.6 = (f32[64,3,1,512]{3,0,2,1:T(8,128)S(1)}, f32[64,3,1,512]{3,0,2,1:T(8,128)S(1)}, u32[]{:S(2)}, u32[]{:S(2)}) collective-permute-start(f32[64,3,1,512]{3,0,2,1:T(8,128)S(1)} %get-tuple-element.62), channel_id=1, source_target_pairs={{0,4},{4,8},{8,12},{1,5},{5,9},{9,13},{2,6},{6,10},{10,14},{3,7},{... | collective-permute-start | bytes 1179656 | tf_op jit(solution)/shard_map/ppermute | solution.py:20
  71.0 9.7 %collective-permute-start.7 = (f32[64,3,1,512]{3,0,2,1:T(8,128)S(1)}, f32[64,3,1,512]{3,0,2,1:T(8,128)S(1)}, u32[]{:S(2)}, u32[]{:S(2)}) collective-permute-start(f32[64,3,1,512]{3,0,2,1:T(8,128)S(1)} %get-tuple-element.63), channel_id=1, source_target_pairs={{4,0},{8,4},{12,8},{5,1},{9,5},{13,9},{6,2},{10,6},{14,10},{7,3},{... | collective-permute-start | bytes 1179656 | tf_op jit(solution)/shard_map/ppermute | solution.py:22
  84.1 0.7 copy-start.4
  84.1 12.6 %copy-start.2 = (f32[1,512]{1,0:T(1,128)S(1)}, f32[1,512]{1,0:T(1,128)}, u32[]{:S(2)}) copy-start(f32[1,512]{1,0:T(1,128)} %param.15) | copy-start | bytes 6148
  84.2 17.0 %copy-start.3 = (f32[1,512]{1,0:T(1,128)S(1)}, f32[1,512]{1,0:T(1,128)}, u32[]{:S(2)}) copy-start(f32[1,512]{1,0:T(1,128)} %param.14) | copy-start | bytes 6148
  87.8 4.4 %collective-permute-start.8 = (f32[64,512]{1,0:T(8,128)S(1)}, f32[64,512]{1,0:T(8,128)S(1)}, u32[]{:S(2)}, u32[]{:S(2)}) collective-permute-start(f32[64,512]{1,0:T(8,128)S(1)} %fusion.3), channel_id=1, source_target_pairs={{0,1},{1,2},{2,3},{3,0},{4,5},{5,6},{6,7},{7,4},{8,9},{9,10},{10,1... | collective-permute-start | bytes 393224 | tf_op jit(solution)/shard_map/ppermute | solution.py:148
  92.2 4.4 %collective-permute-start.9 = (f32[64,512]{1,0:T(8,128)S(1)}, f32[64,512]{1,0:T(8,128)S(1)}, u32[]{:S(2)}, u32[]{:S(2)}) collective-permute-start(f32[64,512]{1,0:T(8,128)S(1)} %collective-permute-done.8), channel_id=1, source_target_pairs={{0,1},{1,2},{2,3},{3,0},{4,5},{5,6},{6,7},{7,4},{8,9},{9,10},{10,1... | collective-permute-start | bytes 393224 | tf_op jit(solution)/shard_map/ppermute | solution.py:148
  96.6 4.4 %collective-permute-start.10 = (f32[64,512]{1,0:T(8,128)S(1)}, f32[64,512]{1,0:T(8,128)S(1)}, u32[]{:S(2)}, u32[]{:S(2)}) collective-permute-start(f32[64,512]{1,0:T(8,128)S(1)} %collective-permute-done.9), channel_id=1, source_target_pairs={{0,1},{1,2},{2,3},{3,0},{4,5},{5,6},{6,7},{7,4},{8,9},{9,10},{10,1... | collective-permute-start | bytes 393224 | tf_op jit(solution)/shard_map/ppermute | solution.py:148
  102.7 75.1 %all-gather.2.cloned.1.call-start = ((), (), s32[]{:S(2)}) async-start(), calls=%async_computation.1 | async-start | bytes 7864320 | tf_op jit(solution)/shard_map/all_gather | solution.py:171
Sparse Core Ops, SparseCore 0:
  102.8 33.6 all-reduce.5
Sparse Core Ops, SparseCore 1:
  104.7 44.5 all-gather.1
